TPU v7x, 1024 devices: a whole 8x8x8 slice. The times are simulated.
1024 devices in a mesh: blk: 32 (over y_hi, z), narrow: 32 (over y_lo, x, core).
Axes of the slice: x: 8, y: 8 (y_hi: 4, y_lo: 2; y = y_hi * 2 + y_lo), z: 8, core: 2. Of those that a mesh axis runs over, the one named last changes fastest.
Arguments:
- factors_a: bfloat16 [2, 2048, 512], replicated, may hold values from -0.25 to 0.25
- factors_b: bfloat16 [512, 2048, 512], P('blk', 'narrow'), may hold values from -0.0078125 to 0.0078125
- amplitudes: bfloat16 [256, 2048, 2048], P('blk', 'narrow'), may hold values from -6 to 6
- screen: int32 [32, 16], replicated, may hold values from 0 to 1, as said below
Outputs:
- residual: float32 [3, 32, 256], P(None, 'blk', 'narrow')
Inputs may be any that keep to these rules, and one draw needn't show every extreme that they name: `screen`: entry [i, s] is 1 where c sub-tile s is kept for pair tile i. Every row keeps 1 to 8 sub-tiles and some row keeps exactly 8.
All inputs are finite; a program needn't handle non-finite values.
Results may differ from a plain program's by a relative error of at most 0.0029.
Values may be sent and summed in bfloat16 or wider, within the bound.
A program may use at most 64 MiB of HBM per device.

v0:
```python
import jax
import jax.numpy as jnp
from jax import lax
from jax.sharding import PartitionSpec as P

CS = 128
STEPS = 3


def passed_along(value, axis, by):
    size = lax.axis_size(axis)
    return lax.ppermute(value, axis, [(i, (i + by) % size) for i in range(size)])


def tile_terms(factors_a, b_panel, screen_row, slab_stack):
    a_rows, virtuals, aux_count = factors_a.shape
    b_rows, d_rows, _ignored = b_panel.shape
    panel_flat = b_panel.reshape(b_rows * d_rows, aux_count)

    def add_tile(sub_at, running):

        def compute(running):
            factor_block = lax.dynamic_slice_in_dim(factors_a, sub_at * CS, CS, 1).reshape(
                a_rows * CS, aux_count
            )
            integral = lax.dot_general(
                factor_block,
                panel_flat,
                (((1,), (1,)), ((), ())),
                preferred_element_type=jnp.float32,
            )
            integral = integral.astype(jnp.bfloat16).reshape(a_rows, CS, b_rows, d_rows)
            amp_block = lax.dynamic_slice_in_dim(slab_stack, sub_at * CS, CS, 2)
            return running + jnp.einsum(
                "xdc,acbd->xab", amp_block, integral, preferred_element_type=jnp.float32
            )

        return lax.cond(screen_row[sub_at] != 0, compute, lambda kept: kept, running)

    initial = jnp.zeros((slab_stack.shape[0], a_rows, b_rows), jnp.float32)
    return lax.fori_loop(0, virtuals // CS, add_tile, initial)


def local(factors_a, factors_b, amplitudes, screen):
    pair_rows = amplitudes.shape[0]
    position = lax.axis_index("blk")
    flat_rows = pair_rows * factors_a.shape[0] * factors_b.shape[0]
    current = amplitudes
    slab_list = [amplitudes]
    for offset in range(1, STEPS):
        current = passed_along(current, "blk", 1)
        slab_list.append(current)
    stacked = jnp.concatenate(slab_list, 0)
    screen_row = lax.dynamic_index_in_dim(screen, position, 0, keepdims=False)
    terms = tile_terms(factors_a, factors_b, screen_row, stacked)
    partial_value = terms.reshape(STEPS, 1, flat_rows)
    summed = lax.psum_scatter(partial_value, "narrow", scatter_dimension=2, tiled=True)
    return summed


def solution(mesh):
    return jax.shard_map(
        local,
        mesh=mesh,
        in_specs=(P(), P("blk", "narrow", None), P("blk", "narrow", None), P()),
        out_specs=P(None, "blk", "narrow"),
        check_vma=False,
    )
```

profile of v0, /device:TPU:32, one launch (start us, length us, event | category | flops | bytes accessed | tf_op | source)
XLA Modules:
  0.0 296.9 jit_solution(17809055079696601012)
XLA Ops:
  0.0 0.0 copy-start
  0.0 2.8 copy.18
  2.8 5.2 %collective-permute-start = (bf16[8,64,2048]{2,0,1:T(8,128)(2,1)S(1)}, bf16[8,64,2048]{2,0,1:T(8,128)(2,1)}, u32[]{:S(2)}, u32[]{:S(2)}) collective-permute-start(bf16[8,64,2048]{2,0,1:T(8,128)(2,1)S(1)} %copy.18), channel_id=1, source_target_pairs={{0,32},{32,64},{64,96},{96,128},{128,160},{160,192},{192,224},{224... | collective-permute-start | bytes 6291464 | tf_op jit(solution)/shard_map/ppermute | solution.py:12
  8.0 80.8 %collective-permute-done = bf16[8,64,2048]{2,0,1:T(8,128)(2,1)} collective-permute-done((bf16[8,64,2048]{2,0,1:T(8,128)(2,1)S(1)}, bf16[8,64,2048]{2,0,1:T(8,128)(2,1)}, u32[]{:S(2)}, u32[]{:S(2)}) %collective-permute-start) | collective-permute-done | bytes 2097184 | tf_op jit(solution)/shard_map/ppermute | solution.py:12
  88.8 1.9 collective-permute-start.1
  90.7 1.3 dynamic-slice
  92.7 0.0 copy-done
  92.7 0.2 dynamic-slice_reduce_fusion
  92.9 0.0 copy-start.1
  92.9 111.3 %collective-permute-done.1 = bf16[8,64,2048]{2,0,1:T(8,128)(2,1)} collective-permute-done((bf16[8,64,2048]{2,0,1:T(8,128)(2,1)}, bf16[8,64,2048]{2,0,1:T(8,128)(2,1)}, u32[]{:S(2)}, u32[]{:S(2)}) %collective-permute-start.1) | collective-permute-done | bytes 2097184 | tf_op jit(solution)/shard_map/ppermute | solution.py:12
  204.2 5.5 %pad_maximum_fusion = bf16[24,64,2048]{2,0,1:T(8,128)(2,1)} fusion(bf16[8,64,2048]{2,0,1:T(8,128)(2,1)} %collective-permute-done.1, bf16[8,64,2048]{2,0,1:T(8,128)(2,1)} %collective-permute-done, bf16[8,64,2048]{2,0,1:T(8,128)(2,1)S(1)} %copy.18), kind=kLoop, calls=%fused_computation.7 | loop fusion | flops 18874368 | bytes 12582912 | tf_op jit(solution)/shard_map/concatenate | solution.py:53
  209.7 0.0 copy-done.1
  209.7 30.2 %while.16 = (s32[]{:T(128)}, f32[24,2,16]{0,2,1:T(8,128)S(1)}, s32[16]{0:T(128)S(1)}, bf16[24,64,2048]{2,0,1:T(8,128)(2,1)}, bf16[2,2048,512]{2,1,0:T(8,128)(2,1...) while((s32[]{:T(128)}, f32[24,2,16]{0,2,1:T(8,128)S(1)}, s32[16]{0:T(128)S(1)}, ...), condition=%wide.region_3.4_spmd, body=%wide.region_0.3_spmd.sunk | while | flops 281281280 | bytes 5380309 | solution.py:41
  209.7 0.7 dynamic_slice.25
  211.0 4.6 %conditional.2 = (f32[24,2,16]{0,2,1:T(8,128)S(1)}) conditional(s32[]{:T(128)} %bitcast.20, f32[24,2,16]{0,2,1:T(8,128)S(1)} %get-tuple-element.196, (s32[]{:T(128)}, bf16[24,64,2048]{2,0,1:T(8,128)(2,1)}, bf16[2,2048,512]{2,1,0:T(8,128)(2,1)}, bf16[1024,512]{1,0:T(8,128)(2,1)S(1)}, f32[24,2,16]{0,2,1:T(8,128)S(1)}) %tuple.39), branch_computations={%region_1.1_spmd, %region_2.2_spmd} | conditional | flops 281281280 | bytes 5380158 | solution.py:38
  211.0 1.0 constant_dynamic-slice_fusion
  212.0 0.5 convolution_convert_fusion
  212.5 0.7 reshape.21
  213.1 1.1 copy.16
  214.3 1.3 fusion
  215.6 0.7 dynamic_slice.25
  216.9 4.6 %conditional.2 = (f32[24,2,16]{0,2,1:T(8,128)S(1)}) conditional(s32[]{:T(128)} %bitcast.20, f32[24,2,16]{0,2,1:T(8,128)S(1)} %get-tuple-element.196, (s32[]{:T(128)}, bf16[24,64,2048]{2,0,1:T(8,128)(2,1)}, bf16[2,2048,512]{2,1,0:T(8,128)(2,1)}, bf16[1024,512]{1,0:T(8,128)(2,1)S(1)}, f32[24,2,16]{0,2,1:T(8,128)S(1)}) %tuple.39), branch_computations={%region_1.1_spmd, %region_2.2_spmd} | conditional | flops 281281280 | bytes 5380158 | solution.py:38
  216.9 1.0 constant_dynamic-slice_fusion
  217.9 0.5 convolution_convert_fusion
  218.3 0.7 reshape.21
  219.0 1.1 copy.16
  220.1 1.3 fusion
  221.5 0.7 dynamic_slice.25
  222.8 0.7 dynamic_slice.25
  224.1 0.7 dynamic_slice.25
  225.4 0.7 dynamic_slice.25
  226.7 0.7 dynamic_slice.25
  228.1 0.7 dynamic_slice.25
  229.4 0.7 dynamic_slice.25
  230.7 0.7 dynamic_slice.25
  232.0 0.7 dynamic_slice.25
  233.4 0.7 dynamic_slice.25
  234.7 0.7 dynamic_slice.25
  236.0 0.7 dynamic_slice.25
  237.3 0.7 dynamic_slice.25
  238.6 0.7 dynamic_slice.25
  240.0 0.1 copy.19
  240.0 0.1 reshape.17
  240.1 56.1 %all-reduce = f32[3,1,256]{2,0,1:T(4,128)S(1)} all-reduce(f32[3,1,256]{2,0,1:T(4,128)S(1)} %reshape.17), channel_id=2, replica_groups=mesh['blk'=32,'narrow'=32] {'narrow'}, use_global_device_ids=true, to_apply=%region_4.5.clone | all-reduce | flops 768 | bytes 6144
  296.3 0.1 constant_dynamic-slice_fusion.1
  296.4 0.6 copy.20
  (15 shorter events, 0.1 us)
Async XLA Ops:
  0.0 92.7 %copy-start = (s32[32,16]{0,1:T(8,128)S(1)}, s32[32,16]{0,1:T(8,128)}, u32[]{:S(2)}) copy-start(s32[32,16]{0,1:T(8,128)} %param.11) | copy-start | bytes 6148
  2.8 86.0 %collective-permute-start = (bf16[8,64,2048]{2,0,1:T(8,128)(2,1)S(1)}, bf16[8,64,2048]{2,0,1:T(8,128)(2,1)}, u32[]{:S(2)}, u32[]{:S(2)}) collective-permute-start(bf16[8,64,2048]{2,0,1:T(8,128)(2,1)S(1)} %copy.18), channel_id=1, source_target_pairs={{0,32},{32,64},{64,96},{96,128},{128,160},{160,192},{192,224},{224... | collective-permute-start | bytes 6291464 | tf_op jit(solution)/shard_map/ppermute | solution.py:12
  88.8 115.4 %collective-permute-start.1 = (bf16[8,64,2048]{2,0,1:T(8,128)(2,1)}, bf16[8,64,2048]{2,0,1:T(8,128)(2,1)}, u32[]{:S(2)}, u32[]{:S(2)}) collective-permute-start(bf16[8,64,2048]{2,0,1:T(8,128)(2,1)} %collective-permute-done), channel_id=1, source_target_pairs={{0,32},{32,64},{64,96},{96,128},{128,160},{160,192},{192,224},{224... | collective-permute-start | bytes 6291464 | tf_op jit(solution)/shard_map/ppermute | solution.py:12
  92.9 116.8 %copy-start.1 = (bf16[16,64,512]{2,1,0:T(8,128)(2,1)S(1)}, bf16[16,64,512]{2,1,0:T(8,128)(2,1)}, u32[]{:S(2)}) copy-start(bf16[16,64,512]{2,1,0:T(8,128)(2,1)} %param.9) | copy-start | bytes 3145732
where the time goes:
time: 300 us; the launch traced here: 297 us
  waiting for transfers between devices  192 us (64%)
  blocking collectives  56.1 us (19%)
  local copies, waits for them, and re-layouts  21 us (7%)
  loops' own time  10.8 us (4%)
  starting transfers between devices  7.1 us (2%)
  other arithmetic  5.51 us (2%)
  matrix products  3.53 us (1%)
    ppermute x2, waiting for transfers between devices, passed_along(): lax.ppermute(value, axis, [(i, (i + by) % size) for i in range(size)])  192 us
    unnamed x1, blocking collectives  56.1 us
    another operation x1, loops' own time, tile_terms(): return lax.fori_loop(0, virtuals // CS, add_tile, initial)  10.6 us
    dynamic_slice x16, local copies, waits for them, and re-layouts, add_tile(): screen_row[sub_at] != 0  10.4 us
    ppermute x2, starting transfers between devices, passed_along(): lax.ppermute(value, axis, [(i, (i + by) % size) for i in range(size)])  7.1 us
  transfers between devices with their start and end apart: 2, of which 2 were waited for; matrix products, arithmetic and copies ran while one was open for 1% of the time, Pallas kernels for 0%

commit v1 on v0

v1 whole, which is shorter than its diff:
```python
import functools

import jax
import jax.numpy as jnp
from jax import lax
from jax.experimental import pallas as pl
from jax.experimental.pallas import tpu as pltpu
from jax.sharding import PartitionSpec as P

MESH = pl.DeviceIdType.MESH
CS = 128
SLOTS = 8
STEPS = 3
DC = 16
NZ = 8
F32 = jnp.float32
BF16 = jnp.bfloat16


def kept_of(screen_ref, row, nsub):
    count = jnp.int32(0)
    at = [jnp.int32(0)] * SLOTS
    for sub in range(nsub):
        count = count + jnp.where(screen_ref[row, sub] != 0, 1, 0)
        at = [a + jnp.where(count <= slot, 1, 0) for slot, a in enumerate(at)]
    return [jnp.minimum(a, nsub - 1) for a in at], count


def kernel(
    n_blk, n_nar, f_hbm, b_hbm, a_hbm, screen_ref, out_ref,
    fv, bv, av, g, gr, br, ak0, ak1, fk0, fk1, integral, acc0, acc1, srow, rrow, fin,
    ld_sem, sb_sem, sa_sem, rb_sem, ra_sem, fwd_sem, rs_send, rs_recv, fin_sem,
):
    blk = lax.axis_index("blk")
    nar = lax.axis_index("narrow")
    n_a, n_virt, n_aux = f_hbm.shape
    n_b, n_d, _ = b_hbm.shape
    n_p = a_hbm.shape[0]
    chunks = n_d // DC
    nsub = n_virt // CS
    z = lax.rem(blk, NZ)
    up = lax.rem(blk + 1, n_blk)
    down = lax.rem(blk + n_blk - 1, n_blk)
    next_ring = lax.rem(blk + NZ, n_blk)
    last_ring = lax.rem(blk + n_blk - NZ, n_blk)
    is_top = lax.div(z + 1, NZ)
    is_low = 1 - lax.div(z + NZ - 1, NZ)

    load_b = pltpu.make_async_copy(b_hbm, bv, ld_sem.at[2])
    for sub in range(nsub):
        pltpu.make_async_copy(a_hbm.at[:, :, sub * CS : (sub + 1) * CS], av.at[sub], ld_sem.at[0]).start()
    for sub in range(nsub):
        pltpu.make_async_copy(f_hbm.at[:, sub * CS : (sub + 1) * CS, :], fv.at[sub], ld_sem.at[1]).start()
    load_b.start()

    barrier = pltpu.get_barrier_semaphore()

    @pl.loop(1, n_nar)
    def _(off):
        pl.semaphore_signal(barrier, inc=1, device_id=(blk, lax.rem(nar + off, n_nar)), device_id_type=MESH)

    for other in (up, down, next_ring, last_ring, blk - z + (NZ - 1 - z)):
        pl.semaphore_signal(barrier, inc=1, device_id=(other, nar), device_id_type=MESH)

    at0, n0 = kept_of(screen_ref, blk, nsub)
    at1, n1 = kept_of(screen_ref, up, nsub)
    at2, _ = kept_of(screen_ref, lax.rem(blk + 2, n_blk), nsub)
    pl.semaphore_wait(barrier, n_nar - 1 + 5)

    hb, hp = n_b // 2, n_p // 2

    def send_b(c, h):
        relay = is_low * h
        return pltpu.make_async_remote_copy(
            src_ref=b_hbm.at[pl.ds(h * hb, hb), pl.ds(c * DC, DC), :],
            dst_ref=br.at[relay, c, pl.ds(h * hb, hb)],
            send_sem=sb_sem,
            recv_sem=rb_sem.at[relay, c],
            device_id=(down * (1 - relay) + (blk + NZ - 1) * relay, nar),
            device_id_type=MESH,
        )

    def send_a(c, h):
        relay = is_top * h
        return pltpu.make_async_remote_copy(
            src_ref=g.at[c, pl.ds(h * hp, hp)],
            dst_ref=gr.at[relay, c, pl.ds(h * hp, hp)],
            send_sem=sa_sem,
            recv_sem=ra_sem.at[relay, c],
            device_id=(up * (1 - relay) + (blk + 1 - NZ) * relay, nar),
            device_id_type=MESH,
        )

    @pl.loop(0, chunks)
    def _(c):
        send_b(c, 1).start()
        send_b(c, 0).start()

    def keep_amps(dst, c, at):
        for slot in range(SLOTS):
            dst[c, :, :, slot * CS : (slot + 1) * CS] = av[at[slot], :, c * DC : (c + 1) * DC, :]

    pltpu.make_async_copy(av, av, ld_sem.at[0]).wait()
    for c in range(chunks):
        keep_amps(g, c, at2)
        send_a(c, 1).start()
        send_a(c, 0).start()

    def relay_on(c):
        @pl.when(z == 0)
        def _():
            here = gr.at[1, c, pl.ds(hp, hp)]
            pltpu.make_async_copy(here, here, ra_sem.at[1, c]).wait()
            pltpu.make_async_remote_copy(
                src_ref=here, dst_ref=gr.at[0, c, pl.ds(hp, hp)], send_sem=fwd_sem, recv_sem=ra_sem.at[0, c],
                device_id=(next_ring, nar), device_id_type=MESH,
            ).start()

        @pl.when(z == NZ - 1)
        def _():
            here = br.at[1, c, pl.ds(hb, hb)]
            pltpu.make_async_copy(here, here, rb_sem.at[1, c]).wait()
            pltpu.make_async_remote_copy(
                src_ref=here, dst_ref=br.at[0, c, pl.ds(hb, hb)], send_sem=fwd_sem, recv_sem=rb_sem.at[0, c],
                device_id=(last_ring, nar), device_id_type=MESH,
            ).start()

    for c in range(chunks):
        keep_amps(ak0, c, at0)
        keep_amps(ak1, c, at1)

    pltpu.make_async_copy(fv, fv, ld_sem.at[1]).wait()
    for fk, at, count in ((fk0, at0, n0), (fk1, at1, n1)):
        for slot in range(SLOTS):
            held = jnp.full((CS, n_aux), jnp.where(slot < count, 1.0, 0.0), F32).astype(BF16)
            for a in range(n_a):
                fk[a, slot * CS : (slot + 1) * CS, :] = fv[at[slot], a] * held
    load_b.wait()
    acc0[...] = jnp.zeros_like(acc0)
    acc1[...] = jnp.zeros_like(acc1)

    def add_chunk(fk, panel, amps, acc):
        for a in range(n_a):
            integral[...] = lax.dot_general(
                fk[a], panel, (((1,), (1,)), ((), ())), preferred_element_type=F32
            ).astype(BF16)
            tile = integral[...]
            for s, amp in enumerate(amps):
                acc[s, a] += jnp.dot(amp, tile, preferred_element_type=F32)

    rows_b, rows_p = n_b * DC, n_p * DC
    relay_on(0)

    @pl.loop(0, chunks)
    def _(c):
        panel = bv[:, pl.ds(pl.multiple_of(c * DC, DC), DC), :].reshape(rows_b, n_aux)
        add_chunk(fk0, panel, (ak0[c].reshape(rows_p, SLOTS * CS),), acc0)

    relay_on(1)

    @pl.loop(0, chunks)
    def _(c):
        @pl.when(c + 2 < chunks)
        def _():
            relay_on(c + 2)

        here = br.at[0, c]
        pltpu.make_async_copy(here, here, rb_sem.at[0, c]).wait()
        here = gr.at[0, c]
        pltpu.make_async_copy(here, here, ra_sem.at[0, c]).wait()
        panel = br[0, c].reshape(rows_b, n_aux)
        amps = (ak1[c].reshape(rows_p, SLOTS * CS), gr[0, c].reshape(rows_p, SLOTS * CS))
        add_chunk(fk1, panel, amps, acc1)

    same_d = lax.rem(lax.broadcasted_iota(jnp.int32, (rows_p, rows_b), 0), DC) == lax.rem(
        lax.broadcasted_iota(jnp.int32, (rows_p, rows_b), 1), DC
    )
    lane = lax.rem(lax.broadcasted_iota(jnp.int32, (n_p, 128), 1), DC)
    halves = rows_b // 128
    for a in range(n_a):
        sums = []
        for acc, s in ((acc0, 0), (acc1, 0), (acc1, 1)):
            kept = jnp.where(same_d, acc[s, a], 0.0)
            sums.append(kept.reshape(n_p, DC, rows_b).sum(axis=1))
        for half in range(halves):
            row = jnp.zeros((n_p, 128), F32)
            for s in range(STEPS):
                part = sums[s][:, half * 128 : (half + 1) * 128]
                for step in (8, 4, 2, 1):
                    part = part + pltpu.roll(part, 128 - step, 1)
                if s:
                    part = pltpu.roll(part, s, 1)
                row = jnp.where(lane == s, part, row)
            for q in range(n_p):
                srow[(q * n_a + a) * halves + half] = row[q : q + 1, :]

    def send_row(off):
        to = lax.rem(nar + off, n_nar)
        return pltpu.make_async_remote_copy(
            src_ref=srow.at[to], dst_ref=rrow.at[nar], send_sem=rs_send, recv_sem=rs_recv,
            device_id=(blk, to), device_id_type=MESH,
        )

    @pl.loop(1, n_nar)
    def _(off):
        send_row(off).start()

    rrow[nar] = srow[nar]
    others = rrow.at[pl.ds(0, n_nar - 1)]
    pltpu.make_async_copy(others, others, rs_recv).wait()
    total = rrow[...].sum(axis=0)
    fin[0] = total
    last = pltpu.make_async_remote_copy(
        src_ref=fin.at[0], dst_ref=fin.at[1], send_sem=fin_sem.at[0], recv_sem=fin_sem.at[1],
        device_id=(up, nar), device_id_type=MESH,
    )
    last.start()
    sent = srow.at[pl.ds(0, n_nar - 1)]
    pltpu.make_async_copy(sent, sent, rs_send).wait()
    pltpu.make_async_copy(g, g, sa_sem).wait()
    pltpu.make_async_copy(b_hbm, b_hbm, sb_sem).wait()

    @pl.when(z == 0)
    def _():
        here = gr.at[1, :, pl.ds(hp, hp)]
        pltpu.make_async_copy(here, here, fwd_sem).wait()

    @pl.when(z == NZ - 1)
    def _():
        here = br.at[1, :, pl.ds(hb, hb)]
        pltpu.make_async_copy(here, here, fwd_sem).wait()

    last.wait()
    out_ref[...] = fin[...]


def local(n_blk, n_nar, factors_a, factors_b, amplitudes, screen):
    n_a, n_virt, n_aux = factors_a.shape
    n_b, n_d, _ = factors_b.shape
    nsub = n_virt // CS
    n_p = amplitudes.shape[0]
    chunks = n_d // DC
    kept = SLOTS * CS
    any_spec = pl.BlockSpec(memory_space=pl.ANY)
    rows = pl.pallas_call(
        functools.partial(kernel, n_blk, n_nar),
        out_shape=jax.ShapeDtypeStruct((2, 1, 128), F32),
        in_specs=[any_spec, any_spec, any_spec, pl.BlockSpec(memory_space=pltpu.SMEM)],
        out_specs=pl.BlockSpec(memory_space=pltpu.VMEM),
        scratch_shapes=[
            pltpu.VMEM((nsub, n_a, CS, n_aux), BF16),
            pltpu.VMEM(factors_b.shape, BF16),
            pltpu.VMEM((nsub, n_p, n_d, CS), BF16),
            pltpu.VMEM((chunks, n_p, DC, kept), BF16),
            pltpu.VMEM((2, chunks, n_p, DC, kept), BF16),
            pltpu.VMEM((2, chunks, n_b, DC, n_aux), BF16),
            pltpu.VMEM((chunks, n_p, DC, kept), BF16),
            pltpu.VMEM((chunks, n_p, DC, kept), BF16),
            pltpu.VMEM((n_a, kept, n_aux), BF16),
            pltpu.VMEM((n_a, kept, n_aux), BF16),
            pltpu.VMEM((kept, n_b * DC), BF16),
            pltpu.VMEM((1, n_a, n_p * DC, n_b * DC), F32),
            pltpu.VMEM((2, n_a, n_p * DC, n_b * DC), F32),
            pltpu.VMEM((n_nar, 1, 128), F32),
            pltpu.VMEM((n_nar, 1, 128), F32),
            pltpu.VMEM((2, 1, 128), F32),
            pltpu.SemaphoreType.DMA((3,)),
            pltpu.SemaphoreType.DMA,
            pltpu.SemaphoreType.DMA,
            pltpu.SemaphoreType.DMA((2, chunks)),
            pltpu.SemaphoreType.DMA((2, chunks)),
            pltpu.SemaphoreType.DMA,
            pltpu.SemaphoreType.DMA,
            pltpu.SemaphoreType.DMA,
            pltpu.SemaphoreType.DMA((2,)),
        ],
        compiler_params=pltpu.CompilerParams(collective_id=0, has_side_effects=True),
        name="ladder",
    )(factors_a, factors_b, amplitudes, screen)
    from_row = jnp.concatenate([rows[:1], rows[1:], rows[1:]], 0)
    step = lax.broadcasted_iota(jnp.int32, (STEPS, 8, 128), 0)
    index = lax.broadcasted_iota(jnp.int32, (STEPS, 8, 128), 1)
    lane = lax.broadcasted_iota(jnp.int32, (STEPS, 8, 128), 2)
    picked = jnp.where(lane == index * DC + step, from_row, 0.0)
    return picked.sum(axis=2).reshape(STEPS, 1, 8)


def solution(mesh):
    return jax.shard_map(
        functools.partial(local, mesh.shape["blk"], mesh.shape["narrow"]),
        mesh=mesh,
        in_specs=(P(), P("blk", "narrow", None), P("blk", "narrow", None), P()),
        out_specs=P(None, "blk", "narrow"),
        check_vma=False,
    )
```

time: 300 us -> 75.1 us (0.25)
  the two profiles are of different devices: /device:TPU:32 before, /device:TPU:1 now
where the time goes in v1:
time: 75.1 us; the launch traced here: 74.8 us
  Pallas kernels  71.4 us (95%)
  local copies, waits for them, and re-layouts  2.6 us (3%)
  other arithmetic  0.82 us (1%)
    pallas_call x1, Pallas kernels, local(): pl.pallas_call(functools.partial(kernel, n_blk, n_nar), out_shape=jax.Sha...  71.4 us

profile of v1, /device:TPU:1, one launch (start us, length us, event | category | flops | bytes accessed | tf_op | source)
XLA Modules:
  0.0 74.8 jit_solution(7675217783948189177)
XLA Ops:
  0.0 1.4 %copy.7.screen_ref = s32[32,16]{1,0:T(8,128)} copy(s32[32,16]{0,1:T(8,128)} %param.7) | data formatting | bytes 4096 | tf_op args[3]
  1.4 71.4 %ladder.1 = f32[2,1,128]{2,1,0:T(1,128)} custom-call(bf16[2,2048,512]{2,1,0:T(8,128)(2,1)} %f_hbm.1, bf16[16,64,512]{2,1,0:T(8,128)(2,1)} %b_hbm.1, bf16[8,64,2048]{2,1,0:T(8,128)(2,1)} %a_hbm.1, s32[32,16]{1,0:T(8,128)} %copy.7.screen_ref), custom_call_target="tpu_custom_call" | custom-call | tf_op jit(solution)/shard_map/ladder/pallas_call | solution.py:245
  72.8 0.7 slice.6
  73.4 0.7 pad_maximum_fusion
  74.1 0.2 select_reduce_fusion
  74.3 0.6 copy.8
  (2 shorter events, 0.0 us)

commit v2 on v1

v2 whole, which is shorter than its diff:
```python
import functools

import jax
import jax.numpy as jnp
from jax import lax
from jax.experimental import pallas as pl
from jax.experimental.pallas import tpu as pltpu
from jax.sharding import PartitionSpec as P

MESH = pl.DeviceIdType.MESH
CS = 128
SLOTS = 8
STEPS = 3
DC = 16
PIECES = 2
RELAYED = 7
NZ = 8
F32 = jnp.float32
BF16 = jnp.bfloat16


def kept_of(screen_ref, row, nsub):
    count = jnp.int32(0)
    at = [jnp.int32(0)] * SLOTS
    for sub in range(nsub):
        count = count + jnp.where(screen_ref[sub, row] != 0, 1, 0)
        at = [a + jnp.where(count <= slot, 1, 0) for slot, a in enumerate(at)]
    return [jnp.minimum(a, nsub - 1) for a in at], count


def kernel(
    n_blk, n_nar, f_hbm, b_hbm, a_hbm, screen_hbm, out_ref,
    screen_ref, fv, bv, av, g, gr, br, ak0, ak1, fk0, fk1, integral, acc0, acc1, srow, rrow, fin,
    ld_sem, sb_sem, sa_sem, rb_sem, ra_sem, fwd_sem, rs_send, rs_recv,
):
    blk = lax.axis_index("blk")
    nar = lax.axis_index("narrow")
    n_a, n_virt, n_aux = f_hbm.shape
    n_b, n_d, _ = b_hbm.shape
    n_p = a_hbm.shape[0]
    chunks = n_d // DC
    nsub = n_virt // CS
    z = lax.rem(blk, NZ)
    up = lax.rem(blk + 1, n_blk)
    down = lax.rem(blk + n_blk - 1, n_blk)
    next_ring = lax.rem(blk + NZ, n_blk)
    last_ring = lax.rem(blk + n_blk - NZ, n_blk)
    is_top = lax.div(z + 1, NZ)
    is_low = 1 - lax.div(z + NZ - 1, NZ)

    barrier = pltpu.get_barrier_semaphore()

    for other in (up, down, next_ring, last_ring, blk - z + (NZ - 1 - z)):
        pl.semaphore_signal(barrier, inc=1, device_id=(other, nar), device_id_type=MESH)

    @pl.loop(1, n_nar)
    def _(off):
        pl.semaphore_signal(barrier, inc=1, device_id=(blk, lax.rem(nar + off, n_nar)), device_id_type=MESH)
        pl.semaphore_signal(barrier, inc=1, device_id=(down, lax.rem(nar + off, n_nar)), device_id_type=MESH)

    load_s = pltpu.make_async_copy(screen_hbm, screen_ref, ld_sem.at[3])
    load_s.start()
    for c in range(chunks):
        pltpu.make_async_copy(b_hbm.at[:, c * DC : (c + 1) * DC, :], bv.at[c], ld_sem.at[2]).start()
    for sub in range(nsub):
        pltpu.make_async_copy(a_hbm.at[:, :, sub * CS : (sub + 1) * CS], av.at[sub], ld_sem.at[0]).start()
    for sub in range(nsub):
        pltpu.make_async_copy(f_hbm.at[:, sub * CS : (sub + 1) * CS, :], fv.at[sub], ld_sem.at[1]).start()
    load_s.wait()
    at0, n0 = kept_of(screen_ref, blk, nsub)
    at1, n1 = kept_of(screen_ref, up, nsub)
    at2, _ = kept_of(screen_ref, lax.rem(blk + 2, n_blk), nsub)

    def keep_amps(dst, c, at):
        for slot in range(SLOTS):
            dst[c, :, :, slot * CS : (slot + 1) * CS] = av[at[slot], :, c * DC : (c + 1) * DC, :]

    pltpu.make_async_copy(av, av, ld_sem.at[0]).wait()
    for c in range(chunks):
        keep_amps(g, c, at2)
    pltpu.make_async_copy(bv, bv, ld_sem.at[2]).wait()
    pl.semaphore_wait(barrier, 2 * (n_nar - 1) + 5)

    hb, hp = n_b // 2, n_p // 2
    qb, qp = hb // PIECES, hp // PIECES

    def send_b(c, first, size, relay, piece):
        return pltpu.make_async_remote_copy(
            src_ref=bv.at[c, pl.ds(first, size)],
            dst_ref=br.at[relay, c, pl.ds(first, size)],
            send_sem=sb_sem,
            recv_sem=rb_sem.at[(c * 2 + first // hb) * (1 - relay) + (chunks * 2 + piece) * relay],
            device_id=(down * (1 - relay) + (blk + NZ - 1) * relay, nar),
            device_id_type=MESH,
        )

    def send_a(c, first, size, relay, piece):
        return pltpu.make_async_remote_copy(
            src_ref=g.at[c, pl.ds(first, size)],
            dst_ref=gr.at[relay, c, pl.ds(first, size)],
            send_sem=sa_sem,
            recv_sem=ra_sem.at[c * (1 - relay) + (chunks + piece) * relay],
            device_id=(up * (1 - relay) + (blk + 1 - NZ) * relay, nar),
            device_id_type=MESH,
        )

    def panels_down():
        @pl.loop(0, chunks)
        def _(c):
            for u in range(PIECES):
                piece = c * PIECES + u
                send_b(c, hb + u * qb, qb, is_low * (1 - lax.div(piece, RELAYED)), piece).start()
            send_b(c, 0, hb, 0, 0).start()

    def amps_up():
        @pl.loop(0, chunks)
        def _(c):
            for u in range(PIECES):
                piece = c * PIECES + u
                send_a(c, hp + u * qp, qp, is_top * (1 - lax.div(piece, RELAYED)), piece).start()
            send_a(c, 0, hp, 0, 0).start()

    @pl.when(z < NZ - 1)
    def _():
        panels_down()
        amps_up()

    @pl.when(z == NZ - 1)
    def _():
        amps_up()
        panels_down()

    def relay_on(piece):
        c, u = lax.div(piece, PIECES), lax.rem(piece, PIECES)

        @pl.when(z == 0)
        def _():
            part = pl.ds(hp + u * qp, qp)
            here = gr.at[1, c, part]
            pltpu.make_async_copy(here, here, ra_sem.at[chunks + piece]).wait()
            pltpu.make_async_remote_copy(
                src_ref=here, dst_ref=gr.at[0, c, part], send_sem=fwd_sem.at[piece], recv_sem=ra_sem.at[c],
                device_id=(next_ring, nar), device_id_type=MESH,
            ).start()

        @pl.when(z == NZ - 1)
        def _():
            part = pl.ds(hb + u * qb, qb)
            here = br.at[1, c, part]
            pltpu.make_async_copy(here, here, rb_sem.at[chunks * 2 + piece]).wait()
            pltpu.make_async_remote_copy(
                src_ref=here, dst_ref=br.at[0, c, part], send_sem=fwd_sem.at[piece], recv_sem=rb_sem.at[c * 2 + 1],
                device_id=(last_ring, nar), device_id_type=MESH,
            ).start()

    for c in range(chunks):
        keep_amps(ak0, c, at0)
        keep_amps(ak1, c, at1)

    pltpu.make_async_copy(fv, fv, ld_sem.at[1]).wait()
    for fk, at, count in ((fk0, at0, n0), (fk1, at1, n1)):
        for slot in range(SLOTS):
            held = jnp.full((CS, n_aux), jnp.where(slot < count, 1.0, 0.0), F32).astype(BF16)
            for a in range(n_a):
                fk[a, slot * CS : (slot + 1) * CS, :] = fv[at[slot], a] * held
    acc0[...] = jnp.zeros_like(acc0)
    acc1[...] = jnp.zeros_like(acc1)

    def integrals(fk, panel, half):
        cols = slice(half * hb * DC, (half + 1) * hb * DC)
        for a in range(n_a):
            integral[a, :, cols] = lax.dot_general(
                fk[a], panel.reshape(hb * DC, n_aux), (((1,), (1,)), ((), ())), preferred_element_type=F32
            ).astype(BF16)

    def add_amps(amps, acc):
        for a in range(n_a):
            tile = integral[a]
            for s, amp in enumerate(amps):
                acc[s, a] += jnp.dot(amp, tile, preferred_element_type=F32)

    rows_b, rows_p = n_b * DC, n_p * DC
    relay_on(0)

    @pl.loop(0, chunks)
    def _(c):
        for half in range(2):
            integrals(fk0, bv[c, half * hb : (half + 1) * hb], half)
        add_amps((ak0[c].reshape(rows_p, SLOTS * CS),), acc0)
        relay_on(c + 1)

    same_d = lax.rem(lax.broadcasted_iota(jnp.int32, (rows_p, rows_b), 0), DC) == lax.rem(
        lax.broadcasted_iota(jnp.int32, (rows_p, rows_b), 1), DC
    )
    lane_s = lax.rem(lax.broadcasted_iota(jnp.int32, (n_p, 128), 1), DC)
    halves = rows_b // 128

    def write_rows(terms, to):
        for a in range(n_a):
            sums = []
            for acc, at, _ in terms:
                kept = jnp.where(same_d, acc[at, a], 0.0)
                sums.append(kept.reshape(n_p, DC, rows_b).sum(axis=1))
            for half in range(halves):
                row = jnp.zeros((n_p, 128), F32)
                for part, (_, _, s) in zip(sums, terms):
                    part = part[:, half * 128 : (half + 1) * 128]
                    for step in (8, 4, 2, 1):
                        part = part + pltpu.roll(part, 128 - step, 1)
                    if s:
                        part = pltpu.roll(part, s, 1)
                    row = jnp.where(lane_s == s, part, row)
                for q in range(n_p):
                    srow[to, (q * n_a + a) * halves + half] = row[q : q + 1, :]

    def send_row(which, tile, off):
        to = lax.rem(nar + off, n_nar)
        return pltpu.make_async_remote_copy(
            src_ref=srow.at[which, to], dst_ref=rrow.at[which, nar], send_sem=rs_send.at[which], recv_sem=rs_recv.at[which],
            device_id=(tile, to), device_id_type=MESH,
        )

    write_rows(((acc0, 0, 0),), 0)

    @pl.loop(1, n_nar)
    def _(off):
        send_row(0, blk, off).start()

    rrow[0, nar] = srow[0, nar]

    @pl.loop(0, chunks)
    def _(c):
        @pl.when(c + chunks + 1 < RELAYED)
        def _():
            relay_on(c + chunks + 1)

        for half in (1, 0):
            here = br.at[0, c, pl.ds(half * hb, hb)]
            pltpu.make_async_copy(here, here, rb_sem.at[c * 2 + half]).wait()
            integrals(fk1, br[0, c, half * hb : (half + 1) * hb], half)
        here = gr.at[0, c]
        pltpu.make_async_copy(here, here, ra_sem.at[c]).wait()
        add_amps((ak1[c].reshape(rows_p, SLOTS * CS), gr[0, c].reshape(rows_p, SLOTS * CS)), acc1)

    write_rows(((acc1, 0, 1), (acc1, 1, 2)), 1)

    @pl.loop(0, n_nar)
    def _(off):
        send_row(1, up, off).start()

    here = rrow.at[0, pl.ds(0, n_nar - 1)]
    pltpu.make_async_copy(here, here, rs_recv.at[0]).wait()
    fin[0] = rrow[0].sum(axis=0)
    pltpu.make_async_copy(rrow.at[1], rrow.at[1], rs_recv.at[1]).wait()
    fin[1] = rrow[1].sum(axis=0)
    sent = srow.at[0, pl.ds(0, n_nar - 1)]
    pltpu.make_async_copy(sent, sent, rs_send.at[0]).wait()
    pltpu.make_async_copy(srow.at[1], srow.at[1], rs_send.at[1]).wait()
    pltpu.make_async_copy(g, g, sa_sem).wait()
    pltpu.make_async_copy(bv, bv, sb_sem).wait()

    @pl.loop(0, RELAYED)
    def _(piece):
        @pl.when(z == 0)
        def _():
            here = gr.at[1, 0, pl.ds(hp, qp)]
            pltpu.make_async_copy(here, here, fwd_sem.at[piece]).wait()

        @pl.when(z == NZ - 1)
        def _():
            here = br.at[1, 0, pl.ds(hb, qb)]
            pltpu.make_async_copy(here, here, fwd_sem.at[piece]).wait()

    step = lax.broadcasted_iota(jnp.int32, (8, 128), 0)
    lane = lax.broadcasted_iota(jnp.int32, (8, 128), 1)
    held = jnp.where(step == 0, fin[0], fin[1])
    spread = jnp.take_along_axis(held, lax.rem(lane * DC + step, 128), axis=1)
    for s in range(STEPS):
        out_ref[s] = spread[s : s + 1, : out_ref.shape[2]]


def local(n_blk, n_nar, factors_a, factors_b, amplitudes, screen):
    n_a, n_virt, n_aux = factors_a.shape
    n_b, n_d, _ = factors_b.shape
    nsub = n_virt // CS
    n_p = amplitudes.shape[0]
    chunks = n_d // DC
    kept = SLOTS * CS
    any_spec = pl.BlockSpec(memory_space=pl.ANY)
    return pl.pallas_call(
        functools.partial(kernel, n_blk, n_nar),
        out_shape=jax.ShapeDtypeStruct((STEPS, 1, n_a * n_b * n_p // n_nar), F32),
        in_specs=[any_spec] * 4,
        out_specs=pl.BlockSpec(memory_space=pltpu.VMEM),
        scratch_shapes=[
            pltpu.SMEM(screen.shape[::-1], jnp.int32),
            pltpu.VMEM((nsub, n_a, CS, n_aux), BF16),
            pltpu.VMEM((chunks, n_b, DC, n_aux), BF16),
            pltpu.VMEM((nsub, n_p, n_d, CS), BF16),
            pltpu.VMEM((chunks, n_p, DC, kept), BF16),
            pltpu.VMEM((2, chunks, n_p, DC, kept), BF16),
            pltpu.VMEM((2, chunks, n_b, DC, n_aux), BF16),
            pltpu.VMEM((chunks, n_p, DC, kept), BF16),
            pltpu.VMEM((chunks, n_p, DC, kept), BF16),
            pltpu.VMEM((n_a, kept, n_aux), BF16),
            pltpu.VMEM((n_a, kept, n_aux), BF16),
            pltpu.VMEM((n_a, kept, n_b * DC), BF16),
            pltpu.VMEM((1, n_a, n_p * DC, n_b * DC), F32),
            pltpu.VMEM((2, n_a, n_p * DC, n_b * DC), F32),
            pltpu.VMEM((2, n_nar, 1, 128), F32),
            pltpu.VMEM((2, n_nar, 1, 128), F32),
            pltpu.VMEM((2, 1, 128), F32),
            pltpu.SemaphoreType.DMA((4,)),
            pltpu.SemaphoreType.DMA,
            pltpu.SemaphoreType.DMA,
            pltpu.SemaphoreType.DMA((chunks * (2 + PIECES),)),
            pltpu.SemaphoreType.DMA((chunks * (1 + PIECES),)),
            pltpu.SemaphoreType.DMA((RELAYED,)),
            pltpu.SemaphoreType.DMA((2,)),
            pltpu.SemaphoreType.DMA((2,)),
        ],
        compiler_params=pltpu.CompilerParams(collective_id=0, has_side_effects=True),
        name="ladder",
    )(factors_a, factors_b, amplitudes, screen.T)


def solution(mesh):
    return jax.shard_map(
        functools.partial(local, mesh.shape["blk"], mesh.shape["narrow"]),
        mesh=mesh,
        in_specs=(P(), P("blk", "narrow", None), P("blk", "narrow", None), P()),
        out_specs=P(None, "blk", "narrow"),
        check_vma=False,
    )
```

time: 75.1 us -> 64.6 us (0.86)
  Pallas kernels: 71.4 us -> 63.2 us
  local copies, waits for them, and re-layouts: 2.6 us -> 1.24 us
  other arithmetic: 0.82 us -> 0 us
    pallas_call x1, Pallas kernels: 71.4 us -> 63.2 us  [local(): pl.pallas_call(functools.partial(kernel, n_blk, n_nar), out_shape=jax.Sha...]
where the time goes in v2:
time: 64.6 us; the launch traced here: 64.5 us
  Pallas kernels  63.2 us (98%)
  local copies, waits for them, and re-layouts  1.24 us (2%)
    pallas_call x1, Pallas kernels, local(): pl.pallas_call(functools.partial(kernel, n_blk, n_nar), out_shape=jax.Sha...  63.2 us

profile of v2, /device:TPU:1, one launch (start us, length us, event | category | flops | bytes accessed | tf_op | source)
XLA Modules:
  0.0 64.5 jit_solution(6184630724346854203)
XLA Ops:
  0.0 63.2 %ladder.1 = f32[3,1,8]{2,1,0:T(1,128)} custom-call(bf16[2,2048,512]{2,1,0:T(8,128)(2,1)} %f_hbm.1, bf16[16,64,512]{2,1,0:T(8,128)(2,1)} %b_hbm.1, bf16[8,64,2048]{2,1,0:T(8,128)(2,1)} %a_hbm.1, s32[16,32]{1,0:T(8,128)} %bitcast.1), custom_call_target="tpu_custom_call" | custom-call | tf_op jit(solution)/shard_map/ladder/pallas_call | solution.py:290
  63.2 1.2 %copy.6 = f32[3,1,8]{2,1,0:T(1,128)} copy(f32[3,1,8]{2,1,0:T(1,128)} %ladder.1) | data formatting | bytes 192

commit v3 on v2

--- a/solution.py
+++ b/solution.py
@@ -13,6 +13,7 @@
 STEPS = 3
 DC = 16
 PIECES = 2
+PER = PIECES // 2 or 1
 RELAYED = 7
 NZ = 8
 F32 = jnp.float32
@@ -60,10 +61,10 @@
 
     load_s = pltpu.make_async_copy(screen_hbm, screen_ref, ld_sem.at[3])
     load_s.start()
+    for sub in range(nsub):
+        pltpu.make_async_copy(a_hbm.at[:, :, sub * CS : (sub + 1) * CS], av.at[sub], ld_sem.at[0]).start()
     for c in range(chunks):
         pltpu.make_async_copy(b_hbm.at[:, c * DC : (c + 1) * DC, :], bv.at[c], ld_sem.at[2]).start()
-    for sub in range(nsub):
-        pltpu.make_async_copy(a_hbm.at[:, :, sub * CS : (sub + 1) * CS], av.at[sub], ld_sem.at[0]).start()
     for sub in range(nsub):
         pltpu.make_async_copy(f_hbm.at[:, sub * CS : (sub + 1) * CS, :], fv.at[sub], ld_sem.at[1]).start()
     load_s.wait()
@@ -166,11 +167,10 @@
     acc0[...] = jnp.zeros_like(acc0)
     acc1[...] = jnp.zeros_like(acc1)
 
-    def integrals(fk, panel, half):
-        cols = slice(half * hb * DC, (half + 1) * hb * DC)
+    def integrals(fk, panel):
         for a in range(n_a):
-            integral[a, :, cols] = lax.dot_general(
-                fk[a], panel.reshape(hb * DC, n_aux), (((1,), (1,)), ((), ())), preferred_element_type=F32
+            integral[a] = lax.dot_general(
+                fk[a], panel.reshape(n_b * DC, n_aux), (((1,), (1,)), ((), ())), preferred_element_type=F32
             ).astype(BF16)
 
     def add_amps(amps, acc):
@@ -180,14 +180,21 @@
                 acc[s, a] += jnp.dot(amp, tile, preferred_element_type=F32)
 
     rows_b, rows_p = n_b * DC, n_p * DC
-    relay_on(0)
+    def relay_step(step):
+        for u in range(PER):
+            piece = step * PER + u
+
+            @pl.when(piece < RELAYED)
+            def _(piece=piece):
+                relay_on(piece)
+
+    relay_step(jnp.int32(0))
 
     @pl.loop(0, chunks)
     def _(c):
-        for half in range(2):
-            integrals(fk0, bv[c, half * hb : (half + 1) * hb], half)
+        integrals(fk0, bv[c])
         add_amps((ak0[c].reshape(rows_p, SLOTS * CS),), acc0)
-        relay_on(c + 1)
+        relay_step(c + 1)
 
     same_d = lax.rem(lax.broadcasted_iota(jnp.int32, (rows_p, rows_b), 0), DC) == lax.rem(
         lax.broadcasted_iota(jnp.int32, (rows_p, rows_b), 1), DC
@@ -230,14 +237,12 @@
 
     @pl.loop(0, chunks)
     def _(c):
-        @pl.when(c + chunks + 1 < RELAYED)
-        def _():
-            relay_on(c + chunks + 1)
+        relay_step(c + chunks + 1)
 
         for half in (1, 0):
             here = br.at[0, c, pl.ds(half * hb, hb)]
             pltpu.make_async_copy(here, here, rb_sem.at[c * 2 + half]).wait()
-            integrals(fk1, br[0, c, half * hb : (half + 1) * hb], half)
+        integrals(fk1, br[0, c])
         here = gr.at[0, c]
         pltpu.make_async_copy(here, here, ra_sem.at[c]).wait()
         add_amps((ak1[c].reshape(rows_p, SLOTS * CS), gr[0, c].reshape(rows_p, SLOTS * CS)), acc1)

time: 64.6 us -> 64.3 us (level)
  no operation moved by 1% of the time
where the time goes in v3:
time: 64.3 us; the launch traced here: 64.1 us
  Pallas kernels  62.9 us (98%)
  local copies, waits for them, and re-layouts  1.24 us (2%)
    pallas_call x1, Pallas kernels, local(): pl.pallas_call(functools.partial(kernel, n_blk, n_nar), out_shape=jax.Sha...  62.9 us

profile of v3, /device:TPU:1, one launch (start us, length us, event | category | flops | bytes accessed | tf_op | source)
XLA Modules:
  0.0 64.1 jit_solution(13234484853111713141)
XLA Ops:
  0.0 62.9 %ladder.1 = f32[3,1,8]{2,1,0:T(1,128)} custom-call(bf16[2,2048,512]{2,1,0:T(8,128)(2,1)} %f_hbm.1, bf16[16,64,512]{2,1,0:T(8,128)(2,1)} %b_hbm.1, bf16[8,64,2048]{2,1,0:T(8,128)(2,1)} %a_hbm.1, s32[16,32]{1,0:T(8,128)} %bitcast.1), custom_call_target="tpu_custom_call" | custom-call | tf_op jit(solution)/shard_map/ladder/pallas_call | solution.py:295
  62.9 1.2 %copy.6 = f32[3,1,8]{2,1,0:T(1,128)} copy(f32[3,1,8]{2,1,0:T(1,128)} %ladder.1) | data formatting | bytes 192
